TPU v7x, 32 devices: a whole 2x2x4 slice. The times are simulated.
32 devices in a mesh: dp: 16 (over z, y, x), mp: 2 (over core).
Axes of the slice: x: 2, y: 2, z: 4, core: 2. Of those that a mesh axis runs over, the one named last changes fastest.
Arguments:
- tokens: bfloat16 [32, 768, 1024], P(('dp', 'mp')), may hold values from -6 to 6
- cotangent: bfloat16 [32, 768, 1024], P(('dp', 'mp')), may hold values from -6 to 6
- class_ids: int32 [32], replicated, may hold values from 0 to 1000
- stop_scales: int32 [32], replicated, may hold values from 7 to 10, as said below
- qkv_weight: bfloat16 [1024, 3, 1024], P(None, None, 'mp'), may hold values from -0.1875 to 0.1875
- query_bias: float32 [1024], P('mp'), may hold values from -3 to 3
- value_bias: float32 [1024], P('mp'), may hold values from -3 to 3
- head_scale: float32 [16], P('mp'), may hold values from 2 to 3
- proj_weight: bfloat16 [1024, 1024], P(None, 'mp'), may hold values from -0.75 to 0.75
- proj_bias: float32 [1024], replicated, may hold values from -1.75 to 1.75
- up_weight: bfloat16 [1024, 4096], P(None, 'mp'), may hold values from -0.1875 to 0.1875
- up_bias: float32 [4096], P('mp'), may hold values from -1.75 to 1.75
- down_weight: bfloat16 [1024, 4096], P(None, 'mp'), may hold values from -0.1875 to 0.1875
- down_bias: float32 [1024], replicated, may hold values from -1.75 to 1.75
- ada_weight: bfloat16 [1024, 6, 1024], replicated, may hold values from -0.1875 to 0.1875
- ada_bias: float32 [1024, 6], replicated, may hold values from -1.75 to 1.75
- class_table: bfloat16 [1024, 1001], replicated, may hold values from -6 to 6
Outputs:
- output: bfloat16 [32, 768, 1024], P(('dp', 'mp'))
- gradient_of_input: bfloat16 [32, 768, 1024], P(('dp', 'mp'))
- qkv_grad: float32 [1024, 3, 1024], P('dp', None, 'mp')
- query_bias_grad: float32 [1024], P('mp')
- value_bias_grad: float32 [1024], P('mp')
- head_scale_grad: float32 [16], P('mp')
- proj_grad: float32 [1024, 1024], P('dp', 'mp')
- proj_bias_grad: float32 [1024], P('dp')
- up_grad: float32 [1024, 4096], P('dp', 'mp')
- up_bias_grad: float32 [4096], P('mp')
- down_grad: float32 [1024, 4096], P('dp', 'mp')
- down_bias_grad: float32 [1024], P('dp')
- ada_grad: float32 [1024, 6, 1024], P('dp')
- ada_bias_grad: float32 [1024, 6], P('dp')
- table_grad: float32 [1024, 1001], P('dp')
Inputs may be any that keep to these rules, and one draw needn't show every extreme that they name: `stop_scales`: each item uses 10 - 3 to 10 token maps, and some item uses all 10.
All inputs are finite; a program needn't handle non-finite values.
Results may differ from a plain program's by a relative error of at most 0.018.
Values may be sent and summed in bfloat16 or wider, within the bound.
No kernel may reach another device: no remote copies, remote signals or barrier semaphores. Data moves between devices by JAX's collectives and lax.ppermute only.
A program may use at most 256 MiB of HBM per device.

v0:
```python
import jax
import jax.numpy as jnp
import numpy as np
from jax import lax
from jax.sharding import PartitionSpec as P

SCALES = 10


side_list = (1, 2, 3, 4, 5, 6, 8, 10, 13, 16)
norm_eps = 1e-06
unit_eps = 1e-06
masked_score = -1e30
highest = lax.Precision.HIGHEST


def scale_limits():
    side_array = np.array(side_list[:SCALES], dtype=np.int64)
    return [int(limit) for limit in np.cumsum(side_array * side_array)]


def scale_number(positions):
    counted = jnp.zeros(positions.shape, jnp.int32)
    for limit in scale_limits():
        counted = counted + (positions >= limit).astype(jnp.int32)
    return counted


def item_lengths(stop_values):
    limits = jnp.array(scale_limits(), dtype=jnp.int32)
    chosen = jnp.arange(SCALES, dtype=jnp.int32)[None, :] == stop_values[:, None] - 1
    return jnp.sum(jnp.where(chosen, limits[None, :], 0), axis=1)


def allowed_mask(row_count, length):
    positions = jnp.arange(row_count, dtype=jnp.int32)
    scales = scale_number(positions)
    return (scales[None, :] <= scales[:, None]) & (positions[None, :] < length)


def norm_rows(values):
    centered = values - jnp.mean(values, axis=-1, keepdims=True)
    spread = jnp.mean(centered * centered, axis=-1, keepdims=True)
    return centered * lax.rsqrt(spread + norm_eps)


def modulate(values, scaling, shifting):
    return norm_rows(values) * (1.0 + scaling[:, None, :]) + shifting[:, None, :]


def unit_heads(values):
    return values * lax.rsqrt(jnp.sum(values * values, axis=-1, keepdims=True) + unit_eps)


def gelu_tanh(values):
    return jax.nn.gelu(values, approximate=True)


def normalize_pair(query_raw, keys_raw, head_scale):
    return (unit_heads(query_raw) * jnp.exp(head_scale)[None, :, None], unit_heads(keys_raw))


def pair_items(values):
    return lax.all_gather(values, "mp", axis=0, tiled=True)


def pair_rows(values):
    return lax.all_gather(values, "mp", axis=0, tiled=True)


def head_total(term, row_count):
    return lax.psum_scatter(
        term(jnp.int32(0), row_count * lax.axis_size("mp")).astype(jnp.bfloat16),
        "mp",
        scatter_dimension=0,
        tiled=True,
    ).astype(jnp.float32)


def unit_total(term, row_count):
    return lax.psum_scatter(
        term(jnp.int32(0), row_count * lax.axis_size("mp")).astype(jnp.bfloat16),
        "mp",
        scatter_dimension=0,
        tiled=True,
    ).astype(jnp.float32)


def attention_item(hidden_rows, length, qkv_weight, query_bias, value_bias, head_scale):
    row_count = hidden_rows.shape[0]
    head_count = head_scale.shape[0]
    projected = jnp.einsum(
        "ld,dko->lko", hidden_rows, qkv_weight, preferred_element_type=jnp.float32
    )
    query_raw = (projected[:, 0] + query_bias).reshape(row_count, head_count, -1)
    keys_raw = projected[:, 1].reshape(row_count, head_count, -1)
    values = (projected[:, 2] + value_bias).reshape(row_count, head_count, -1).astype(jnp.bfloat16)
    query_low = (unit_heads(query_raw) * jnp.exp(head_scale)[None, :, None]).astype(jnp.bfloat16)
    keys_low = unit_heads(keys_raw).astype(jnp.bfloat16)
    scores = jnp.einsum("qhd,khd->hqk", query_low, keys_low, preferred_element_type=jnp.float32)
    scores = jnp.where(allowed_mask(row_count, length)[None], scores, masked_score)
    largest = jnp.max(scores, axis=2, keepdims=True)
    exponent = jnp.exp(scores - largest)
    row_sum = jnp.sum(exponent, axis=2, keepdims=True)
    softmax_low = (exponent / row_sum).astype(jnp.bfloat16)
    joined = jnp.einsum("hqk,khd->qhd", softmax_low, values, preferred_element_type=jnp.float32)
    joined = joined.reshape(row_count, -1).astype(jnp.bfloat16)
    return (joined, query_raw, keys_raw, values, largest + jnp.log(row_sum))


def attention_item_back(
    grad_rows, query_raw, keys_raw, values, log_total, length, proj_weight, head_scale
):
    row_count = query_raw.shape[0]
    head_count = query_raw.shape[1]
    grad_joined = jnp.einsum(
        "lo,oj->lj", grad_rows, proj_weight, preferred_element_type=jnp.float32
    )
    grad_joined = grad_joined.astype(jnp.bfloat16).reshape(row_count, head_count, -1)
    unit_pair, normalize_backward = jax.vjp(normalize_pair, query_raw, keys_raw, head_scale)
    query_low = unit_pair[0].astype(jnp.bfloat16)
    keys_low = unit_pair[1].astype(jnp.bfloat16)
    scores = jnp.einsum("qhd,khd->hqk", query_low, keys_low, preferred_element_type=jnp.float32)
    scores = jnp.where(allowed_mask(row_count, length)[None], scores, masked_score)
    softmax_full = jnp.exp(scores - log_total)
    grad_soft = jnp.einsum("qhd,khd->hqk", grad_joined, values, preferred_element_type=jnp.float32)
    grad_values = jnp.einsum(
        "hqk,qhd->khd",
        softmax_full.astype(jnp.bfloat16),
        grad_joined,
        preferred_element_type=jnp.float32,
    ).astype(jnp.bfloat16)
    inner = jnp.sum(softmax_full * grad_soft, axis=2, keepdims=True)
    grad_scores = (softmax_full * (grad_soft - inner)).astype(jnp.bfloat16)
    lowered_query_gradient = jnp.einsum(
        "hqk,khd->qhd", grad_scores, keys_low, preferred_element_type=jnp.float32
    )
    lowered_key_gradient = jnp.einsum(
        "hqk,qhd->khd", grad_scores, query_low, preferred_element_type=jnp.float32
    )
    query_rows_gradient, key_rows_gradient, scale_gradient_total = normalize_backward(
        (lowered_query_gradient, lowered_key_gradient)
    )
    grad_projected = jnp.stack(
        [
            query_rows_gradient.astype(jnp.bfloat16).reshape(row_count, -1),
            key_rows_gradient.astype(jnp.bfloat16).reshape(row_count, -1),
            grad_values.reshape(row_count, -1),
        ],
        axis=1,
    )
    return (grad_projected, scale_gradient_total)


def forward_pass(tokens_wide, modulation, pair_lengths, weights):
    (
        qkv_weight,
        query_bias,
        value_bias,
        head_scale,
        proj_weight,
        proj_bias,
        up_weight,
        up_bias,
        down_weight,
        down_bias,
    ) = weights
    first_in = modulate(tokens_wide, modulation[:, 2], modulation[:, 4]).astype(jnp.bfloat16)
    item_rows = pair_items(first_in)

    def one_item(packed):
        return attention_item(packed[0], packed[1], qkv_weight, query_bias, value_bias, head_scale)

    joined, query_raw, keys_raw, values, log_total = lax.map(one_item, (item_rows, pair_lengths))

    def project(offset, amount):
        return jnp.einsum("ilj,oj->ilo", joined, proj_weight, preferred_element_type=jnp.float32)

    branch = head_total(project, tokens_wide.shape[0])
    branch = (branch + proj_bias).astype(jnp.bfloat16)
    middle = tokens_wide + modulation[:, 0][:, None, :] * branch.astype(jnp.float32)
    second_in = modulate(middle, modulation[:, 3], modulation[:, 5]).astype(jnp.bfloat16)
    rows_all = pair_rows(second_in)
    hidden_pre = (
        jnp.einsum("ipd,df->ipf", rows_all, up_weight, preferred_element_type=jnp.float32) + up_bias
    )
    hidden = gelu_tanh(hidden_pre).astype(jnp.bfloat16)

    def lower(offset, amount):
        return jnp.einsum("ipf,of->ipo", hidden, down_weight, preferred_element_type=jnp.float32)

    mlp_out = unit_total(lower, tokens_wide.shape[0]) + down_bias
    return (
        item_rows,
        joined,
        query_raw,
        keys_raw,
        values,
        log_total,
        branch,
        middle,
        rows_all,
        hidden_pre,
        hidden,
        mlp_out,
    )


def per_device(
    tokens,
    cotangent,
    class_ids,
    stop_scales,
    qkv_weight,
    query_bias,
    value_bias,
    head_scale,
    proj_weight,
    proj_bias,
    up_weight,
    up_bias,
    down_weight,
    down_bias,
    ada_weight,
    ada_bias,
    class_table,
):
    pair_count = lax.axis_size("mp")
    pair_index = lax.axis_index("mp")
    data_index = lax.axis_index("dp")
    local_items = tokens.shape[0]
    slot_count = tokens.shape[1]
    all_items = class_ids.shape[0]
    classes = class_table.shape[1]
    item_ids = jnp.arange(all_items, dtype=jnp.int32)
    all_lengths = item_lengths(stop_scales)
    pair_first = data_index * pair_count * local_items
    own_first = pair_first + pair_index * local_items
    own_items = own_first + jnp.arange(local_items, dtype=jnp.int32)
    own_lengths = jnp.sum(
        jnp.where(own_items[:, None] == item_ids[None, :], all_lengths[None, :], 0), axis=1
    )
    paired = pair_first + jnp.arange(pair_count * local_items, dtype=jnp.int32)
    pair_lengths = jnp.sum(
        jnp.where(paired[:, None] == item_ids[None, :], all_lengths[None, :], 0), axis=1
    )
    class_hot = (class_ids[:, None] == jnp.arange(classes, dtype=jnp.int32)[None, :]).astype(
        jnp.bfloat16
    )
    cond_all = jnp.einsum("bc,dc->bd", class_hot, class_table, preferred_element_type=jnp.float32)
    lifted_all = jax.nn.silu(cond_all).astype(jnp.bfloat16)
    lifted_own = lax.dynamic_slice_in_dim(lifted_all, own_first, local_items, 0)
    modulation = (
        jnp.einsum("bi,iko->bko", lifted_own, ada_weight, preferred_element_type=jnp.float32)
        + ada_bias.T[None]
    )
    tokens_wide = tokens.astype(jnp.float32)
    weights = (
        qkv_weight,
        query_bias,
        value_bias,
        head_scale,
        proj_weight,
        proj_bias,
        up_weight,
        up_bias,
        down_weight,
        down_bias,
    )
    forward_state = forward_pass(tokens_wide, modulation, pair_lengths, weights)
    output = (forward_state[7] + modulation[:, 1][:, None, :] * forward_state[11]).astype(
        jnp.bfloat16
    )
    forward_state = forward_pass(tokens_wide, modulation, pair_lengths, weights)
    (
        item_rows,
        joined,
        query_raw,
        keys_raw,
        values,
        log_total,
        branch,
        middle,
        rows_all,
        hidden_pre,
        hidden,
        mlp_out,
    ) = forward_state
    positions = jnp.arange(slot_count, dtype=jnp.int32)
    live = (positions[None, :] < own_lengths[:, None]).astype(jnp.float32)
    grad_out = cotangent.astype(jnp.float32) * live[:, :, None]
    grad_gamma_two = jnp.sum(grad_out * mlp_out, axis=1)
    grad_mlp = (grad_out * modulation[:, 1][:, None, :]).astype(jnp.bfloat16)
    grad_rows = pair_rows(grad_mlp)
    grad_hidden = jnp.einsum(
        "ipo,of->ipf", grad_rows, down_weight, preferred_element_type=jnp.float32
    )
    unused_gelu, gelu_back = jax.vjp(gelu_tanh, hidden_pre)
    grad_pre = gelu_back(grad_hidden)[0].astype(jnp.bfloat16)
    down_part = jnp.einsum("ipo,ipf->of", grad_rows, hidden, preferred_element_type=jnp.float32)
    down_bias_part = jnp.sum(grad_rows.astype(jnp.float32), axis=(0, 1))
    up_part = jnp.einsum("ipd,ipf->df", rows_all, grad_pre, preferred_element_type=jnp.float32)
    up_bias_part = jnp.sum(grad_pre.astype(jnp.float32), axis=(0, 1))

    def raise_back(offset, amount):
        return jnp.einsum("ipf,df->ipd", grad_pre, up_weight, preferred_element_type=jnp.float32)

    grad_second = unit_total(raise_back, local_items)
    unused_second, second_back = jax.vjp(modulate, middle, modulation[:, 3], modulation[:, 5])
    grad_middle, grad_scale_two, grad_shift_two = second_back(grad_second)
    grad_middle = grad_middle + grad_out
    grad_gamma_one = jnp.sum(grad_middle * branch.astype(jnp.float32), axis=1)
    grad_branch = (grad_middle * modulation[:, 0][:, None, :]).astype(jnp.bfloat16)
    grad_items = pair_items(grad_branch)
    proj_bias_part = jnp.sum(grad_items.astype(jnp.float32), axis=(0, 1))
    proj_part = jnp.einsum("ilo,ilj->oj", grad_items, joined, preferred_element_type=jnp.float32)

    def back_item(packed):
        return attention_item_back(
            packed[0],
            packed[1],
            packed[2],
            packed[3],
            packed[4],
            packed[5],
            proj_weight,
            head_scale,
        )

    grad_projected, scale_parts = lax.map(
        back_item, (grad_items, query_raw, keys_raw, values, log_total, pair_lengths)
    )
    head_scale_part = jnp.sum(scale_parts, axis=0)
    query_bias_part = jnp.sum(grad_projected[:, :, 0].astype(jnp.float32), axis=(0, 1))
    value_bias_part = jnp.sum(grad_projected[:, :, 2].astype(jnp.float32), axis=(0, 1))
    qkv_part = jnp.einsum(
        "ild,ilko->dko", item_rows, grad_projected, preferred_element_type=jnp.float32
    )

    def lower_back(offset, amount):
        return jnp.einsum(
            "ilko,dko->ild", grad_projected, qkv_weight, preferred_element_type=jnp.float32
        )

    grad_first = head_total(lower_back, local_items)
    grad_first = grad_first.astype(jnp.bfloat16).astype(jnp.float32)
    unused_first, first_back = jax.vjp(modulate, tokens_wide, modulation[:, 2], modulation[:, 4])
    grad_tokens, grad_scale_one, grad_shift_one = first_back(grad_first)
    gradient_of_input = (grad_middle + grad_tokens).astype(jnp.bfloat16)
    grad_mod = jnp.stack(
        [
            grad_gamma_one,
            grad_gamma_two,
            grad_scale_one,
            grad_scale_two,
            grad_shift_one,
            grad_shift_two,
        ],
        axis=1,
    )
    grad_mod_pair = lax.all_gather(grad_mod, "mp", axis=0, tiled=True)
    bias_totals = lax.psum((query_bias_part, value_bias_part, head_scale_part, up_bias_part), "dp")
    pair_total = pair_count * local_items
    lifted_pair = lax.dynamic_slice_in_dim(lifted_all, pair_first, pair_total, 0).astype(
        jnp.float32
    )
    cond_pair = lax.dynamic_slice_in_dim(cond_all, pair_first, pair_total, 0)
    hot_pair = lax.dynamic_slice_in_dim(class_hot, pair_first, pair_total, 0).astype(jnp.float32)
    ada_part = jnp.einsum(
        "bi,bko->iko",
        lifted_pair,
        grad_mod_pair,
        precision=highest,
        preferred_element_type=jnp.float32,
    )
    ada_bias_part = jnp.sum(grad_mod_pair, axis=0).T
    grad_lifted = jnp.einsum(
        "bko,iko->bi",
        grad_mod_pair,
        ada_weight.astype(jnp.float32),
        precision=highest,
        preferred_element_type=jnp.float32,
    )
    unused_silu, silu_back = jax.vjp(jax.nn.silu, cond_pair)
    grad_cond = silu_back(grad_lifted)[0]
    table_part = jnp.einsum(
        "bd,bc->dc", grad_cond, hot_pair, precision=highest, preferred_element_type=jnp.float32
    )
    summed = (
        lax.psum_scatter(qkv_part, "dp", scatter_dimension=0, tiled=True),
        lax.psum_scatter(proj_part, "dp", scatter_dimension=0, tiled=True),
        lax.psum_scatter(proj_bias_part, "dp", scatter_dimension=0, tiled=True),
        lax.psum_scatter(up_part, "dp", scatter_dimension=0, tiled=True),
        lax.psum_scatter(down_part, "dp", scatter_dimension=0, tiled=True),
        lax.psum_scatter(down_bias_part, "dp", scatter_dimension=0, tiled=True),
        lax.psum_scatter(ada_part, "dp", scatter_dimension=0, tiled=True),
        lax.psum_scatter(ada_bias_part, "dp", scatter_dimension=0, tiled=True),
        lax.psum_scatter(table_part, "dp", scatter_dimension=0, tiled=True),
    )
    (
        qkv_grad,
        proj_grad,
        proj_bias_grad,
        up_grad,
        down_grad,
        down_bias_grad,
        ada_grad,
        ada_bias_grad,
        table_grad,
    ) = summed
    query_bias_grad, value_bias_grad, head_scale_grad, up_bias_grad = bias_totals
    return (
        output,
        gradient_of_input,
        qkv_grad,
        query_bias_grad,
        value_bias_grad,
        head_scale_grad,
        proj_grad,
        proj_bias_grad,
        up_grad,
        up_bias_grad,
        down_grad,
        down_bias_grad,
        ada_grad,
        ada_bias_grad,
        table_grad,
    )


def solution(mesh):
    return jax.shard_map(
        per_device,
        mesh=mesh,
        in_specs=(
            P(("dp", "mp"), None, None),
            P(("dp", "mp"), None, None),
            P(),
            P(),
            P(None, None, "mp"),
            P("mp"),
            P("mp"),
            P("mp"),
            P(None, "mp"),
            P(),
            P(None, "mp"),
            P("mp"),
            P(None, "mp"),
            P(),
            P(),
            P(),
            P(),
        ),
        out_specs=(
            P(("dp", "mp"), None, None),
            P(("dp", "mp"), None, None),
            P("dp", None, "mp"),
            P("mp"),
            P("mp"),
            P("mp"),
            P("dp", "mp"),
            P("dp"),
            P("dp", "mp"),
            P("mp"),
            P("dp", "mp"),
            P("dp"),
            P("dp", None, None),
            P("dp", None),
            P("dp", None),
        ),
        check_vma=False,
    )
```

profile of v0, /device:TPU:0, one launch (start us, length us, event | category | flops | bytes accessed | tf_op | source)
XLA Modules:
  0.0 1659.9 jit_solution(5937280106903985986)
XLA Ops:
  38.0 78.5 %while.47 = (s32[]{:T(128)}, bf16[2,768,512]{1,2,0:T(8,128)(2,1)}, f32[2,768,8,64]{1,3,2,0:T(8,128)}, f32[2,768,8,64]{1,3,2,0:T(8,128)}, bf16[2,768,8,64]{1,3,2,...) while((s32[]{:T(128)}, bf16[2,768,512]{1,2,0:T(8,128)(2,1)}, ...), condition=%wide.region_20.21_spmd, body=%wide.region_15.20_spmd.sunk | while | flops 3674227200 | bytes 122316592 | solution.py:174
  121.8 12.4 reduce-scatter.20.cloned.1.call-done
  146.0 97.3 %while.46 = (s32[]{:T(128)}, bf16[2,768,512]{1,2,0:T(8,128)(2,1)}, bf16[2,768,1024]{2,1,0:T(8,128)(2,1)}, bf16[1024,3,512]{0,2,1:T(8,128)(2,1)}, f32[512]{0:T(51...) while((s32[]{:T(128)}, bf16[2,768,512]{1,2,0:T(8,128)(2,1)}, ...), condition=%wide.region_9.10_spmd, body=%wide.region_4.0_spmd.sunk | while | flops 3658898688 | bytes 124917480 | solution.py:174
  163.7 22.6 %fusion.238 = (f32[8,768]{1,0:T(8,128)S(1)}, f32[8,768,768]{1,2,0:T(8,128)}) fusion(f32[8,768,768]{1,2,0:T(8,128)} %fusion.237, pred[768,768]{0,1:T(8,128)(4,1)S(1)} %compare_and_fusion.6), kind=kOutput, calls=%fused_computation.310.clone.1 | output fusion | flops 18875136 | bytes 38363136 | tf_op jit(solution)/shard_map/while/body/eval_jaxpr/sub | solution.py:103
  212.6 21.1 %fusion.238 = (f32[8,768]{1,0:T(8,128)S(1)}, f32[8,768,768]{1,2,0:T(8,128)}) fusion(f32[8,768,768]{1,2,0:T(8,128)} %fusion.237, pred[768,768]{0,1:T(8,128)(4,1)S(1)} %compare_and_fusion.6), kind=kOutput, calls=%fused_computation.310.clone.1 | output fusion | flops 18875136 | bytes 38363136 | tf_op jit(solution)/shard_map/while/body/eval_jaxpr/sub | solution.py:103
  248.6 12.3 fusion.96
  260.9 19.8 %convert_reduce_fusion = (f32[2048]{0:T(1024)}, bf16[2,768,2048]{2,1,0:T(8,128)(2,1)S(1)}) fusion(f32[2,768,2048]{2,1,0:T(8,128)} %fusion.96, f32[2048]{0:T(1024)S(1)} %copy-done.66, bf16[2,768,1024]{2,1,0:T(8,128)(2,1)} %all-gather.10.cloned.1.call-done, bf16[1024,2048]{1,0:T(8,128)(2,1)} %param.36), kind=kOutput, calls=%fused_computation.168 | convolution fusion | flops 6514800640 | bytes 26230784 | tf_op jit(solution)/shard_map/ipo,of->ipf/dot_general | solution.py:295
  292.2 13.4 fusion.126
  330.9 12.8 all-gather.14.cloned.1.call-done
  343.6 140.1 %while.48 = (s32[]{:T(128)}, bf16[2,768,3,512]{1,3,2,0:T(8,128)(2,1)}, f32[2,8]{1,0:T(2,128)S(1)}, f32[2,768,8,64]{1,3,2,0:T(8,128)}, s32[2]{0:T(128)S(1)}, /*in...) while((s32[]{:T(128)}, ...), condition=%wide.region_34.35_spmd, body=%wide.region_27.34_spmd.sunk | while | flops 3903902208 | bytes 192113680 | solution.py:330
  372.3 13.0 multiply_reduce_fusion.17
  385.3 13.0 multiply_convert_fusion.25
  441.9 13.0 multiply_reduce_fusion.17
  454.9 13.0 multiply_convert_fusion.25
  527.8 13.0 convolution_bitcast_fusion
  540.9 11.8 convolution_bitcast_fusion.1
  563.4 12.7 convolution_bitcast_fusion.3
  580.8 14.1 fusion.140
  604.2 77.5 %all-reduce.2 = (f32[512]{0:T(512)}, f32[512]{0:T(512)}, f32[8]{0:T(128)}, f32[1024]{0:T(1024)S(1)}, f32[2048]{0:T(1024)}, /*index=5*/f32[1024]{0:T(1024)S(1)}) all-reduce(f32[512]{0:T(512)S(1)} %get-tuple-element.457, f32[512]{0:T(512)S(1)} %get-tuple-element.456, f32[8]{0:T(128)S(1)} %reduce_sum.451, ...), channel_id=1, replica_groups=mesh['dp'=16,'mp'=2] {'dp'}, use_global_device_ids=true, to_apply=%region_40.41 | all-reduce | flops 5128 | bytes 41024 | tf_op jit(solution)/shard_map/psum | solution.py:362
  690.5 173.5 %reduce-scatter.32.cloned.1.call-done = f32[64,2048]{1,0:T(8,128)} async-done(((f32[1024,2048]{1,0:T(8,128)}), f32[64,2048]{1,0:T(8,128)}) %reduce-scatter.32.cloned.1.call-update) | async-done | bytes 524304 | tf_op jit(solution)/shard_map/reduce_scatter | solution.py:394
  864.1 183.1 %reduce-scatter.30.cloned.1.call-done = f32[64,2048]{1,0:T(8,128)} async-done(((f32[1024,2048]{1,0:T(8,128)}), f32[64,2048]{1,0:T(8,128)}) %reduce-scatter.30.cloned.1.call-update) | async-done | bytes 524304 | tf_op jit(solution)/shard_map/reduce_scatter | solution.py:393
  1047.1 141.4 %reduce-scatter.26.cloned.1.call-done = f32[64,3,512]{2,0,1:T(8,128)} async-done(((f32[1024,3,512]{2,0,1:T(8,128)}), f32[64,3,512]{2,0,1:T(8,128)}) %reduce-scatter.26.cloned.1.call-update) | async-done | bytes 393232 | tf_op jit(solution)/shard_map/reduce_scatter | solution.py:390
  1188.5 99.3 %reduce-scatter.38.cloned.1.call-done = f32[64,1001]{1,0:T(8,128)} async-done(((f32[1024,1001]{1,0:T(8,128)}), f32[64,1001]{1,0:T(8,128)}) %reduce-scatter.38.cloned.1.call-update) | async-done | bytes 256272 | tf_op jit(solution)/shard_map/reduce_scatter | solution.py:398
  1287.9 365.0 %reduce-scatter.36.cloned.1.call-done = f32[64,6,1024]{2,0,1:T(8,128)} async-done(((f32[1024,6,1024]{2,0,1:T(8,128)}), f32[64,6,1024]{2,0,1:T(8,128)}) %reduce-scatter.36.cloned.1.call-update) | async-done | bytes 1572880 | tf_op jit(solution)/shard_map/reduce_scatter | solution.py:396
  (384 shorter events, 384.2 us)
Async XLA Ops:
  7.2 29.5 %all-gather.6.cloned.1.call-start = ((), (), s32[]{:S(2)}) async-start(), calls=%async_computation.13 | async-start | bytes 4718592 | tf_op jit(solution)/shard_map/all_gather | solution.py:64
  21.7 112.5 %reduce-scatter.20.cloned.1.call-start = ((), (), s32[]{:S(2)}) async-start(), calls=%async_computation.18 | async-start | bytes 4718592 | tf_op jit(solution)/shard_map/reduce_scatter | solution.py:72
  121.8 126.8 %all-gather.12.cloned.1.call-start = ((), (), s32[]{:S(2)}) async-start(), calls=%async_computation.19 | async-start | bytes 4718592 | tf_op jit(solution)/shard_map/all_gather | solution.py:68
  140.3 120.7 %all-gather.10.cloned.1.call-start = ((), (), s32[]{:S(2)}) async-start(), calls=%async_computation.17 | async-start | bytes 4718592 | tf_op jit(solution)/shard_map/all_gather | solution.py:68
  144.6 161.1 %reduce-scatter.16.cloned.1.call-start = ((), (), s32[]{:S(2)}) async-start(), calls=%async_computation.14 | async-start | bytes 4718592 | tf_op jit(solution)/shard_map/reduce_scatter | solution.py:72
  163.7 22.6 %copy-start.9 = (f32[768,1,512]{0,2,1:T(8,128)S(1)}, f32[768,1,512]{0,2,1:T(8,128)}, u32[]{:S(2)}) copy-start(f32[768,1,512]{0,2,1:T(8,128)} %get-tuple-element.781) | copy-start | bytes 4718596 | tf_op jit(solution)/shard_map/while
  248.5 57.2 %reduce-scatter.22.cloned.1.call-start = ((), (), s32[]{:S(2)}) async-start(), calls=%async_computation.20 | async-start | bytes 4718592 | tf_op jit(solution)/shard_map/reduce_scatter | solution.py:81
  292.1 27.3 %reduce-scatter.34.cloned.1.call-start = ((), (), s32[]{:S(2)}) async-start(), calls=%async_computation.27 | async-start | bytes 4718592 | tf_op jit(solution)/shard_map/reduce_scatter | solution.py:81
  305.7 37.9 %all-gather.14.cloned.1.call-start = ((), (), s32[]{:S(2)}) async-start(), calls=%async_computation.21 | async-start | bytes 4718592 | tf_op jit(solution)/shard_map/all_gather | solution.py:64
  330.1 163.3 %all-gather.8.cloned.1.call-start = ((), (), s32[]{:S(2)}) async-start(), calls=%async_computation.15 | async-start | bytes 4718592 | tf_op jit(solution)/shard_map/all_gather | solution.py:68
  330.8 181.9 %reduce-scatter.24.cloned.1.call-start = ((), (), s32[]{:S(2)}) async-start(), calls=%async_computation.22 | async-start | bytes 4718592 | tf_op jit(solution)/shard_map/reduce_scatter | solution.py:72
  493.3 189.6 %reduce-scatter.18.cloned.1.call-start = ((), (), s32[]{:S(2)}) async-start(), calls=%async_computation.16 | async-start | bytes 4718592 | tf_op jit(solution)/shard_map/reduce_scatter | solution.py:81
  512.6 176.5 %reduce-scatter.40.cloned.1.call-start = ((), (), s32[]{:S(2)}) async-start(), calls=%async_computation.30 | async-start | bytes 557056
  521.6 168.9 %reduce-scatter.28.cloned.1.call-start = ((), (), s32[]{:S(2)}) async-start(), calls=%async_computation.24 | async-start | bytes 2228224 | tf_op jit(solution)/shard_map/reduce_scatter | solution.py:391
  527.7 336.4 %reduce-scatter.32.cloned.1.call-start = ((), (), s32[]{:S(2)}) async-start(), calls=%async_computation.26 | async-start | bytes 8912896 | tf_op jit(solution)/shard_map/reduce_scatter | solution.py:394
  540.8 506.3 %reduce-scatter.30.cloned.1.call-start = ((), (), s32[]{:S(2)}) async-start(), calls=%async_computation.25 | async-start | bytes 8912896 | tf_op jit(solution)/shard_map/reduce_scatter | solution.py:393
  552.7 635.8 %reduce-scatter.26.cloned.1.call-start = ((), (), s32[]{:S(2)}) async-start(), calls=%async_computation.23 | async-start | bytes 6684672 | tf_op jit(solution)/shard_map/reduce_scatter | solution.py:390
  562.6 725.2 %reduce-scatter.38.cloned.1.call-start = ((), (), s32[]{:S(2)}) async-start(), calls=%async_computation.29 | async-start | bytes 4456448 | tf_op jit(solution)/shard_map/reduce_scatter | solution.py:398
  580.7 1072.1 %reduce-scatter.36.cloned.1.call-start = ((), (), s32[]{:S(2)}) async-start(), calls=%async_computation.28 | async-start | bytes 26738688 | tf_op jit(solution)/shard_map/reduce_scatter | solution.py:396
  599.3 83.6 %copy-start.21 = (f32[1,1,1024]{2,1,0:T(1,128)S(1)}, f32[1,1,1024]{2,1,0:T(1,128)}, u32[]{:S(2)}) copy-start(f32[1,1,1024]{2,1,0:T(1,128)} %get-tuple-element.570) | copy-start | bytes 12292
  599.3 83.6 %copy-start.28 = (f32[1024]{0:T(1024)S(1)}, f32[1024]{0:T(1024)}, u32[]{:S(2)}) copy-start(f32[1024]{0:T(1024)} %param.33) | copy-start | bytes 12292
  599.3 83.6 %copy-start.43 = (f32[1,1,1024]{2,1,0:T(1,128)S(1)}, f32[1,1,1024]{2,1,0:T(1,128)}, u32[]{:S(2)}) copy-start(f32[1,1,1024]{2,1,0:T(1,128)} %get-tuple-element.565) | copy-start | bytes 12292
  599.3 83.6 %copy-start.56 = (f32[1024]{0:T(1024)S(1)}, f32[1024]{0:T(1024)}, u32[]{:S(2)}) copy-start(f32[1024]{0:T(1024)} %param.37) | copy-start | bytes 12292
  682.9 969.9 %copy-start.1 = (bf16[1024,1001]{0,1:T(8,128)(2,1)S(1)}, bf16[1024,1001]{0,1:T(8,128)(2,1)}, u32[]{:S(2)}) copy-start(bf16[1024,1001]{0,1:T(8,128)(2,1)} %param.40) | copy-start | bytes 6150148
  (78 other events, 470.2 us)
Sparse Core Ops, SparseCore 0:
  21.8 14.8 all-gather.5
  121.9 12.3 reduce-scatter.19
  140.4 13.3 all-gather.11
  155.2 13.2 all-gather.9
  248.7 12.4 reduce-scatter.15
  292.2 12.4 reduce-scatter.21
  307.0 12.4 reduce-scatter.33
  330.2 13.3 all-gather.13
  345.7 13.2 all-gather.7
  493.4 12.3 reduce-scatter.23
  512.7 12.3 reduce-scatter.17
  527.2 78.8 reduce-scatter.39
  609.0 77.9 reduce-scatter.27
  689.7 174.3 reduce-scatter.31
  866.8 180.3 reduce-scatter.29
  1049.9 138.5 reduce-scatter.25
  1191.2 96.5 reduce-scatter.37
  1294.0 358.7 reduce-scatter.35
where the time goes:
time: 1660 us
  waiting for transfers between devices  999 us (60%)
  matrix products  351 us (21%)
  other arithmetic  178 us (11%)
  blocking collectives  79.5 us (5%)
  local copies, waits for them, and re-layouts  34.3 us (2%)
    reduce_scatter x1, waiting for transfers between devices, per_device(): lax.psum_scatter(ada_part, 'dp', scatter_dimension=0, tiled=True)  365 us
    reduce_scatter x1, waiting for transfers between devices, per_device(): lax.psum_scatter(up_part, 'dp', scatter_dimension=0, tiled=True)  183 us
    reduce_scatter x1, waiting for transfers between devices, per_device(): lax.psum_scatter(down_part, 'dp', scatter_dimension=0, tiled=True)  174 us
    reduce_scatter x1, waiting for transfers between devices, per_device(): lax.psum_scatter(qkv_part, 'dp', scatter_dimension=0, tiled=True)  141 us
    reduce_scatter x1, waiting for transfers between devices, per_device(): lax.psum_scatter(table_part, 'dp', scatter_dimension=0, tiled=True)  99.3 us
    psum x1, blocking collectives, per_device(): lax.psum((query_bias_part, value_bias_part, head_scale_part, up_bias_part...  77.5 us
    sub x2, other arithmetic, attention_item(): exponent = jnp.exp(scores - largest)  43.7 us
    dot_general x4, matrix products, attention_item(): jnp.einsum('hqk,khd->qhd', softmax_low, values, preferred_element_type=jn...  34.8 us
  transfers between devices with their start and end apart: 18, of which 9 were waited for; matrix products, arithmetic and copies ran while one was open for 26% of the time, Pallas kernels for 0%

commit v1 on v0

v1 whole, which is shorter than its diff:
```python
import jax
import jax.numpy as jnp
import numpy as np
from jax import lax
from jax.sharding import PartitionSpec as P

SCALES = 10
side_list = (1, 2, 3, 4, 5, 6, 8, 10, 13, 16)
norm_eps = 1e-06
unit_eps = 1e-06
masked_score = -1e30
highest = lax.Precision.HIGHEST
bf16 = jnp.bfloat16
f32 = jnp.float32


def scale_limits():
    side_array = np.array(side_list[:SCALES], dtype=np.int64)
    return [int(limit) for limit in np.cumsum(side_array * side_array)]


def scale_number(positions):
    counted = jnp.zeros(positions.shape, jnp.int32)
    for limit in scale_limits():
        counted = counted + (positions >= limit).astype(jnp.int32)
    return counted


def item_lengths(stop_values):
    limits = jnp.array(scale_limits(), dtype=jnp.int32)
    chosen = jnp.arange(SCALES, dtype=jnp.int32)[None, :] == stop_values[:, None] - 1
    return jnp.sum(jnp.where(chosen, limits[None, :], 0), axis=1)


def allowed_mask(row_count, length):
    positions = jnp.arange(row_count, dtype=jnp.int32)
    scales = scale_number(positions)
    return (scales[None, :] <= scales[:, None]) & (positions[None, :] < length)


def norm_rows(values):
    centered = values - jnp.mean(values, axis=-1, keepdims=True)
    spread = jnp.mean(centered * centered, axis=-1, keepdims=True)
    inverse = lax.rsqrt(spread + norm_eps)
    return centered * inverse, inverse


def norm_back(grad, scaling, normal, inverse):
    scaled = grad * (1.0 + scaling)
    return inverse * (
        scaled
        - jnp.mean(scaled, axis=-1, keepdims=True)
        - normal * jnp.mean(scaled * normal, axis=-1, keepdims=True)
    )


def unit_heads(values):
    return values * lax.rsqrt(jnp.sum(values * values, axis=-1, keepdims=True) + unit_eps)


def gelu_tanh(values):
    return jax.nn.gelu(values, approximate=True)


def normalize_pair(query_raw, keys_raw, head_scale):
    return (unit_heads(query_raw) * jnp.exp(head_scale)[None, :, None], unit_heads(keys_raw))


def dot(left, right, left_axis, right_axis):
    return lax.dot_general(
        left, right, (((left_axis,), (right_axis,)), ((), ())), preferred_element_type=f32
    )


def swap_pair(values):
    return lax.ppermute(values, "mp", [(0, 1), (1, 0)])


def attention_front(query_raw, keys_raw, values, head_scale, length):
    rows = query_raw.shape[0]
    heads = head_scale.shape[0]
    query_raw = query_raw.reshape(rows, heads, -1)
    keys_raw = keys_raw.reshape(rows, heads, -1)
    values = values.reshape(rows, heads, -1)
    query_low = (unit_heads(query_raw) * jnp.exp(head_scale)[None, :, None]).astype(bf16)
    keys_low = unit_heads(keys_raw).astype(bf16)
    scores = jnp.einsum("qhd,khd->hqk", query_low, keys_low, preferred_element_type=f32)
    scores = jnp.where(allowed_mask(rows, length)[None], scores, masked_score)
    largest = jnp.max(scores, axis=2, keepdims=True)
    exponent = jnp.exp(scores - largest)
    row_sum = jnp.sum(exponent, axis=2, keepdims=True)
    softmax_low = (exponent / row_sum).astype(bf16)
    joined = jnp.einsum("hqk,khd->qhd", softmax_low, values, preferred_element_type=f32)
    return joined.reshape(rows, -1).astype(bf16), largest + jnp.log(row_sum)


def attention_back(grad_joined, query_raw, keys_raw, values, log_total, head_scale, length):
    rows = query_raw.shape[0]
    heads = head_scale.shape[0]
    grad_joined = grad_joined.reshape(rows, heads, -1)
    query_raw = query_raw.reshape(rows, heads, -1)
    keys_raw = keys_raw.reshape(rows, heads, -1)
    values = values.reshape(rows, heads, -1)
    unit_pair, normalize_backward = jax.vjp(normalize_pair, query_raw, keys_raw, head_scale)
    query_low = unit_pair[0].astype(bf16)
    keys_low = unit_pair[1].astype(bf16)
    scores = jnp.einsum("qhd,khd->hqk", query_low, keys_low, preferred_element_type=f32)
    scores = jnp.where(allowed_mask(rows, length)[None], scores, masked_score)
    softmax_full = jnp.exp(scores - log_total)
    grad_soft = jnp.einsum("qhd,khd->hqk", grad_joined, values, preferred_element_type=f32)
    grad_values = jnp.einsum(
        "hqk,qhd->khd", softmax_full.astype(bf16), grad_joined, preferred_element_type=f32
    ).astype(bf16)
    inner = jnp.sum(softmax_full * grad_soft, axis=2, keepdims=True)
    grad_scores = (softmax_full * (grad_soft - inner)).astype(bf16)
    query_part = jnp.einsum("hqk,khd->qhd", grad_scores, keys_low, preferred_element_type=f32)
    key_part = jnp.einsum("hqk,qhd->khd", grad_scores, query_low, preferred_element_type=f32)
    grad_query, grad_keys, grad_scale = normalize_backward((query_part, key_part))
    return (
        grad_query.astype(bf16).reshape(rows, -1),
        grad_keys.astype(bf16).reshape(rows, -1),
        grad_values.reshape(rows, -1),
        grad_scale,
    )


def scatter_rows(values, axis):
    return lax.psum_scatter(values, "dp", scatter_dimension=axis, tiled=True)


def per_device(
    tokens,
    cotangent,
    class_ids,
    stop_scales,
    qkv_weight,
    query_bias,
    value_bias,
    head_scale,
    proj_weight,
    proj_bias,
    up_weight,
    up_bias,
    down_weight,
    down_bias,
    ada_weight,
    ada_bias,
    class_table,
):
    pair_count = lax.axis_size("mp")
    data_count = lax.axis_size("dp")
    pair_index = lax.axis_index("mp")
    data_index = lax.axis_index("dp")
    slots, width = tokens.shape[1:]
    items = class_ids.shape[0]
    classes = class_table.shape[1]
    own_rows = width // data_count
    row_first = data_index * own_rows
    own = data_index * pair_count + pair_index
    half_heads = head_scale.shape[0]
    half_width = query_bias.shape[0]
    half_units = up_bias.shape[0]

    qkv_own = jnp.transpose(qkv_weight, (1, 0, 2))
    attn_own = jnp.concatenate([qkv_own, proj_weight[None]], axis=0)
    attn_other = swap_pair(attn_own)
    small_own = jnp.concatenate([query_bias, value_bias, up_bias, head_scale])
    small_other = swap_pair(small_own)
    up_other = swap_pair(up_weight)
    down_other = swap_pair(down_weight)
    cuts = np.cumsum([half_width, half_width, half_units]).tolist()
    query_bias_other, value_bias_other, up_bias_other, head_scale_other = jnp.split(
        small_other, cuts
    )
    attn_halves = (
        (qkv_own, proj_weight, query_bias, value_bias, head_scale),
        (attn_other[:3], attn_other[3], query_bias_other, value_bias_other, head_scale_other),
    )
    unit_halves = (
        (up_weight, up_bias, down_weight),
        (up_other, up_bias_other, down_other),
    )

    lengths = item_lengths(stop_scales)
    length = jnp.sum(jnp.where(jnp.arange(items, dtype=jnp.int32) == own, lengths, 0))
    class_hot = (class_ids[:, None] == jnp.arange(classes, dtype=jnp.int32)[None, :]).astype(bf16)
    cond_all = jnp.einsum("bc,dc->bd", class_hot, class_table, preferred_element_type=f32)
    lifted_all = jax.nn.silu(cond_all).astype(bf16)
    lifted_own = lax.dynamic_slice_in_dim(lifted_all, own, 1, 0)
    modulation = (
        jnp.einsum("bi,iko->bko", lifted_own, ada_weight, preferred_element_type=f32)[0]
        + ada_bias.T
    )
    gamma_one, gamma_two, scale_one, scale_two, shift_one, shift_two = [
        modulation[k : k + 1] for k in range(6)
    ]

    tokens_wide = tokens[0].astype(f32)
    normal_one, inverse_one = norm_rows(tokens_wide)
    first = (normal_one * (1.0 + scale_one) + shift_one).astype(bf16)
    attn_saved = []
    branch = proj_bias[None]
    for qkv_half, proj_half, qb, vb, hs in attn_halves:
        query_raw = dot(first, qkv_half[0], 1, 0) + qb
        keys_raw = dot(first, qkv_half[1], 1, 0)
        values = (dot(first, qkv_half[2], 1, 0) + vb).astype(bf16)
        joined, log_total = attention_front(query_raw, keys_raw, values, hs, length)
        attn_saved.append((query_raw, keys_raw, values, joined, log_total))
        branch = branch + dot(joined, proj_half, 1, 1)
    branch = branch.astype(bf16)
    middle = tokens_wide + gamma_one * branch.astype(f32)
    normal_two, inverse_two = norm_rows(middle)
    second = (normal_two * (1.0 + scale_two) + shift_two).astype(bf16)
    unit_saved = []
    mlp_out = down_bias[None]
    for up_half, ub, down_half in unit_halves:
        pre = dot(second, up_half, 1, 0) + ub
        hidden = gelu_tanh(pre).astype(bf16)
        unit_saved.append((pre, hidden))
        mlp_out = mlp_out + dot(hidden, down_half, 1, 1)
    output = (middle + gamma_two * mlp_out).astype(bf16)

    live = (jnp.arange(slots, dtype=jnp.int32) < length).astype(f32)
    grad_out = cotangent[0].astype(f32) * live[:, None]
    grad_gamma_two = jnp.sum(grad_out * mlp_out, axis=0)
    grad_mlp = (grad_out * gamma_two).astype(bf16)
    down_bias_part = jnp.sum(grad_mlp.astype(f32), axis=0)
    grad_pres = []
    grad_second = None
    for (up_half, ub, down_half), (pre, hidden) in zip(unit_halves, unit_saved):
        grad_hidden = dot(grad_mlp, down_half, 1, 0)
        grad_pre = jax.vjp(gelu_tanh, pre)[1](grad_hidden)[0].astype(bf16)
        grad_pres.append(grad_pre)
        part = dot(grad_pre, up_half, 1, 1)
        grad_second = part if grad_second is None else grad_second + part
    up_bias_parts = [jnp.sum(g.astype(f32), axis=0) for g in grad_pres]
    down_got = swap_pair(dot(grad_mlp, unit_saved[1][1], 0, 0).astype(bf16))
    down_part = (dot(grad_mlp, unit_saved[0][1], 0, 0) + down_got.astype(f32)).astype(bf16)
    down_grad = scatter_rows(down_part, 0).astype(f32)
    up_got = swap_pair(dot(second, grad_pres[1], 0, 0).astype(bf16))
    up_part = (dot(second, grad_pres[0], 0, 0) + up_got.astype(f32)).astype(bf16)
    up_grad = scatter_rows(up_part, 0).astype(f32)

    grad_scale_two = jnp.sum(grad_second * normal_two, axis=0)
    grad_shift_two = jnp.sum(grad_second, axis=0)
    grad_middle = grad_out + norm_back(grad_second, scale_two, normal_two, inverse_two)
    grad_gamma_one = jnp.sum(grad_middle * branch.astype(f32), axis=0)
    grad_branch = (grad_middle * gamma_one).astype(bf16)
    proj_bias_part = jnp.sum(grad_branch.astype(f32), axis=0)
    proj_got = swap_pair(dot(grad_branch, attn_saved[1][3], 0, 0).astype(bf16))
    proj_part = (dot(grad_branch, attn_saved[0][3], 0, 0) + proj_got.astype(f32)).astype(bf16)
    proj_grad = scatter_rows(proj_part, 0).astype(f32)

    def ordered(parts):
        lower = jnp.where(pair_index == 0, parts[0], parts[1])
        upper = jnp.where(pair_index == 0, parts[1], parts[0])
        return jnp.concatenate([lower, upper])

    def gather_items(vectors):
        packed = jnp.concatenate(vectors)
        count = packed.shape[0]
        padded = -(-count // 1024) * 1024
        packed = jnp.pad(packed, (0, padded - count)).reshape(1, padded // 128, 128)
        gathered = lax.all_gather(packed, ("dp", "mp"), axis=0, tiled=True)
        return gathered.reshape(items, padded)

    early = gather_items(
        [
            grad_gamma_one,
            grad_gamma_two,
            grad_scale_two,
            grad_shift_two,
            down_bias_part,
            proj_bias_part,
            ordered(up_bias_parts),
        ]
    )

    back = []
    grad_first = None
    for (qkv_half, proj_half, qb, vb, hs), (query_raw, keys_raw, values, joined, log_total) in zip(
        attn_halves, attn_saved
    ):
        grad_joined = dot(grad_branch, proj_half, 1, 0).astype(bf16)
        grads = attention_back(grad_joined, query_raw, keys_raw, values, log_total, hs, length)
        back.append(grads)
        for kind in range(3):
            part = dot(grads[kind], qkv_half[kind], 1, 1)
            grad_first = part if grad_first is None else grad_first + part
    qkv_sent = jnp.stack([dot(first, back[1][kind], 0, 0).astype(bf16) for kind in range(3)])
    qkv_got = swap_pair(qkv_sent)
    qkv_part = jnp.stack(
        [
            (dot(first, back[0][kind], 0, 0) + qkv_got[kind].astype(f32)).astype(bf16)
            for kind in range(3)
        ]
    )
    qkv_grad = jnp.transpose(scatter_rows(qkv_part, 1), (1, 0, 2)).astype(f32)
    grad_first = grad_first.astype(bf16).astype(f32)
    grad_scale_one = jnp.sum(grad_first * normal_one, axis=0)
    grad_shift_one = jnp.sum(grad_first, axis=0)
    gradient_of_input = (
        grad_middle + norm_back(grad_first, scale_one, normal_one, inverse_one)
    ).astype(bf16)
    late = gather_items(
        [
            grad_scale_one,
            grad_shift_one,
            ordered([jnp.sum(b[0].astype(f32), axis=0) for b in back]),
            ordered([jnp.sum(b[2].astype(f32), axis=0) for b in back]),
            ordered([b[3] for b in back]),
        ]
    )

    early_sum = jnp.sum(early[:, 4 * width :], axis=0)
    late_sum = jnp.sum(late[:, 2 * width :], axis=0)

    def pair_slice(values, amount):
        return lax.dynamic_slice_in_dim(values, pair_index * amount, amount, 0)

    def data_slice(values):
        return lax.dynamic_slice_in_dim(values, row_first, own_rows, 0)

    down_bias_grad = data_slice(early_sum[:width])
    proj_bias_grad = data_slice(early_sum[width : 2 * width])
    up_bias_grad = pair_slice(early_sum[2 * width : 2 * width + 2 * half_units], half_units)
    query_bias_grad = pair_slice(late_sum[:width], half_width)
    value_bias_grad = pair_slice(late_sum[width : 2 * width], half_width)
    head_scale_grad = pair_slice(late_sum[2 * width : 2 * width + 2 * half_heads], half_heads)
    grad_mod = jnp.stack(
        [
            early[:, :width],
            early[:, width : 2 * width],
            late[:, :width],
            early[:, 2 * width : 3 * width],
            late[:, width : 2 * width],
            early[:, 3 * width : 4 * width],
        ],
        axis=1,
    )
    lifted_rows = lax.dynamic_slice_in_dim(lifted_all, row_first, own_rows, 1).astype(f32)
    cond_rows = lax.dynamic_slice_in_dim(cond_all, row_first, own_rows, 1)
    ada_rows = lax.dynamic_slice_in_dim(ada_weight, row_first, own_rows, 0).astype(f32)
    ada_grad = jnp.einsum(
        "bi,bko->iko", lifted_rows, grad_mod, precision=highest, preferred_element_type=f32
    )
    ada_bias_grad = lax.dynamic_slice_in_dim(jnp.sum(grad_mod, axis=0), row_first, own_rows, 1).T
    grad_lifted = jnp.einsum(
        "bko,iko->bi", grad_mod, ada_rows, precision=highest, preferred_element_type=f32
    )
    grad_cond = jax.vjp(jax.nn.silu, cond_rows)[1](grad_lifted)[0]
    table_grad = jnp.einsum(
        "bd,bc->dc",
        grad_cond,
        class_hot.astype(f32),
        precision=highest,
        preferred_element_type=f32,
    )
    return (
        output[None],
        gradient_of_input[None],
        qkv_grad,
        query_bias_grad,
        value_bias_grad,
        head_scale_grad,
        proj_grad,
        proj_bias_grad,
        up_grad,
        up_bias_grad,
        down_grad,
        down_bias_grad,
        ada_grad,
        ada_bias_grad,
        table_grad,
    )


def solution(mesh):
    return jax.shard_map(
        per_device,
        mesh=mesh,
        in_specs=(
            P(("dp", "mp"), None, None),
            P(("dp", "mp"), None, None),
            P(),
            P(),
            P(None, None, "mp"),
            P("mp"),
            P("mp"),
            P("mp"),
            P(None, "mp"),
            P(),
            P(None, "mp"),
            P("mp"),
            P(None, "mp"),
            P(),
            P(),
            P(),
            P(),
        ),
        out_specs=(
            P(("dp", "mp"), None, None),
            P(("dp", "mp"), None, None),
            P("dp", None, "mp"),
            P("mp"),
            P("mp"),
            P("mp"),
            P("dp", "mp"),
            P("dp"),
            P("dp", "mp"),
            P("mp"),
            P("dp", "mp"),
            P("dp"),
            P("dp", None, None),
            P("dp", None),
            P("dp", None),
        ),
        check_vma=False,
    )
```

time: 1660 us -> 694 us (0.42)
  waiting for transfers between devices: 999 us -> 254 us
  other arithmetic: 178 us -> 78.8 us
  matrix products: 351 us -> 269 us
  blocking collectives: 79.5 us -> 45.2 us
    reduce_scatter x12 -> x4, waiting for transfers between devices: 976 us -> 240 us  [scatter_rows(): return lax.psum_scatter(values, 'dp', scatter_dimension=axis, tiled=True)]
    dot_general x41 -> x52, matrix products: 344 us -> 262 us  [the longest x36 147 us: dot(): lax.dot_general(left, right, (((left_axis,), (right_axis,)), ((), ())), p...]
    psum x1 -> x0, blocking collectives: 77.5 us -> none  [per_device(): lax.psum((query_bias_part, value_bias_part, head_scale_part, up_bias_part...]
    sub x2 -> x0, other arithmetic: 43.7 us -> none  [attention_item(): exponent = jnp.exp(scores - largest)]
    all_gather x1, blocking collectives: 1.91 us -> 45.2 us  [gather_items(): gathered = lax.all_gather(packed, ('dp', 'mp'), axis=0, tiled=True)]
    reduce_sum x26 -> x9, other arithmetic: 58.1 us -> 20.2 us  [the longest x1 16 us: attention_front(): row_sum = jnp.sum(exponent, axis=2, keepdims=True)]
    all_gather x5 -> x1, waiting for transfers between devices: 21.6 us -> 0.01 us  [gather_items(): gathered = lax.all_gather(packed, ('dp', 'mp'), axis=0, tiled=True)]
    convert_element_type x10 -> x12, other arithmetic: 48.5 us -> 41 us  [the longest x1 25.2 us: attention_back(): grad_scores = (softmax_full * (grad_soft - inner)).astype(bf16)]
  transfers between devices with their start and end apart: 18 -> 13, of which waited for: 9 -> 6; matrix products, arithmetic and copies ran while one was open for 26% -> 29% of each run, Pallas kernels for 0% -> 0%
where the time goes in v1:
time: 694 us; the launch traced here: 691 us
  matrix products  269 us (39%)
  waiting for transfers between devices  254 us (37%)
  other arithmetic  78.8 us (11%)
  blocking collectives  45.2 us (7%)
  local copies, waits for them, and re-layouts  22.9 us (3%)
  between operations  17.6 us (3%)
    reduce_scatter x4, waiting for transfers between devices, scatter_rows(): return lax.psum_scatter(values, 'dp', scatter_dimension=axis, tiled=True)  240 us
    dot_general x36, matrix products, dot(): lax.dot_general(left, right, (((left_axis,), (right_axis,)), ((), ())), p...  147 us
    all_gather x1, blocking collectives, gather_items(): gathered = lax.all_gather(packed, ('dp', 'mp'), axis=0, tiled=True)  45.2 us
    dot_general x2, matrix products, attention_back(): jnp.einsum('qhd,khd->hqk', grad_joined, values, preferred_element_type=f32)  35.7 us
    convert_element_type x1, other arithmetic, attention_back(): grad_scores = (softmax_full * (grad_soft - inner)).astype(bf16)  25.2 us
    dot_general x2, matrix products, attention_front(): jnp.einsum('qhd,khd->hqk', query_low, keys_low, preferred_element_type=f32)  21 us
    dot_general x2, matrix products, attention_back(): jnp.einsum('hqk,qhd->khd', softmax_full.astype(bf16), grad_joined, prefer...  20.6 us
    reduce_sum x1, other arithmetic, attention_front(): row_sum = jnp.sum(exponent, axis=2, keepdims=True)  16 us
  transfers between devices with their start and end apart: 13, of which 6 were waited for; matrix products, arithmetic and copies ran while one was open for 29% of the time, Pallas kernels for 0%

profile of v1, /device:TPU:0, one launch (start us, length us, event | category | flops | bytes accessed | tf_op | source)
XLA Modules:
  0.0 690.6 jit_solution(398358277759232960)
XLA Ops:
  23.0 6.4 fusion.167
  34.9 7.9 %fusion.140 = f32[8,768,768]{1,2,0:T(8,128)} fusion(f32[768,8,64]{0,2,1:T(8,128)S(1)} %get-tuple-element.67, f32[768,8]{0,1:T(8,128)S(1)} %get-tuple-element.93, f32[8]{0:T(128)S(1)} %exp.29, f32[768,8]{0,1:T(8,128)S(1)} %get-tuple-element.94, f32[768,512]{0,1:T(8,128)S(1)} %get-tuple-element.69), kind=kOutput, calls=%fused_computation.216 | convolution fusion | flops 605945856 | bytes 22069280 | tf_op jit(solution)/shard_map/qhd,khd->hqk/dot_general | solution.py:87
  54.5 13.1 %select_reduce_fusion = (f32[8,768]{1,0:T(8,128)S(1)}, f32[8,768]{1,0:T(8,128)S(1)}, f32[8,768,768]{1,2,0:T(8,128)}) fusion(pred[768,768]{0,1:T(8,128)(4,1)S(1)} %compare_and_fusion, f32[8,768,768]{1,2,0:T(8,128)} %fusion.140, f32[768,8,64]{0,2,1:T(8,128)S(1)} %get-tuple-element.71, f32[768,8]{0,1:T(8,128)S(1)} %add_rsqrt_fusion, ...), kind=kOutput, calls=%fused_computation.12 | convolution fusion | flops 624807936 | bytes 41582624 | tf_op jit(solution)/shard_map/qhd,khd->hqk/dot_general | solution.py:87
  67.7 16.0 %fusion.1 = (f32[8,768]{1,0:T(8,128)S(1)}, f32[8,768]{1,0:T(8,128)S(1)}) fusion(f32[8,768,768]{1,2,0:T(8,128)} %get-tuple-element.74, f32[8,768]{1,0:T(8,128)S(1)} %get-tuple-element.33, pred[768,768]{0,1:T(8,128)(4,1)S(1)} %compare_and_fusion, f32[8,768]{1,0:T(8,128)S(1)} %get-tuple-element.34, f32[8,768,768]{1,2,0:T(8,128)} %fusion.140), kind=kLoop, calls=%fused_computation.11 | loop fusion | flops 28299264 | bytes 38436864 | tf_op jit(solution)/shard_map/reduce_sum | solution.py:91
  83.7 9.2 %fusion.108 = bf16[8,64,768]{2,1,0:T(8,128)(2,1)S(1)} fusion(bf16[768,8,64]{0,2,1:T(8,128)(2,1)S(1)} %bitcast.427, f32[8,768,768]{1,2,0:T(8,128)} %fusion.140, f32[8,768]{1,0:T(8,128)S(1)} %get-tuple-element.32, f32[8,768]{1,0:T(8,128)S(1)} %get-tuple-element.34, pred[768,768]{0,1:T(8,128)(4,1)S(1)} %compare_and_fusion), kind=kOutput, calls=%fused_computation.176 | convolution fusion | flops 623247360 | bytes 21086208 | tf_op jit(solution)/shard_map/hqk,khd->qhd/dot_general | solution.py:93
  112.4 7.0 %fusion.220 = f32[768,2048]{1,0:T(8,128)S(1)} fusion(bf16[768,1024]{1,0:T(8,128)(2,1)S(1)} %add_convert_fusion.4, bf16[1024,2048]{1,0:T(8,128)(2,1)} %collective-permute-done.2), kind=kOutput, calls=%fused_computation.332 | convolution fusion | flops 3221225472 | bytes 12058624 | tf_op jit(solution)/shard_map/dot_general | solution.py:70
  119.4 11.2 %convert_reduce_fusion.1 = (f32[2048]{0:T(1024)}, bf16[768,2048]{1,0:T(8,128)(2,1)S(1)}) fusion(f32[768,2048]{1,0:T(8,128)S(1)} %fusion.219, f32[2048]{0:T(1024)S(1)} %copy-done.72, bf16[1024,2048]{1,0:T(8,128)(2,1)} %param.30, bf16[1,768,1024]{2,1,0:T(8,128)(2,1)S(1)} %copy-done.90, f32[768]{0:T(1024)S(1)} %fusion.175, f32[1024]{0:T(1024)S(1)} %bitcast.461), kind=kOutput, calls=%fused_computation.43 | convolution fusion | flops 3260545024 | bytes 15227904 | tf_op jit(solution)/shard_map/dot_general | solution.py:70
  137.7 8.0 %fusion.184 = f32[768,1024]{1,0:T(8,128)} fusion(bf16[1024,2048]{1,0:T(8,128)(2,1)} %param.30, f32[768,2048]{1,0:T(8,128)S(1)} %fusion.219, f32[2048]{0:T(1024)S(1)} %copy-done.72), kind=kOutput, calls=%fused_computation.323 | convolution fusion | flops 3236954112 | bytes 13639680 | tf_op jit(solution)/shard_map/dot_general | solution.py:70
  145.7 10.8 %convert_reduce_fusion = (f32[2048]{0:T(1024)S(1)}, bf16[768,2048]{1,0:T(8,128)(2,1)}) fusion(f32[768,2048]{1,0:T(8,128)S(1)} %fusion.220, f32[2048]{0:T(1024)S(1)} %split.19, bf16[1024,2048]{1,0:T(8,128)(2,1)} %collective-permute-done.3, bf16[1,768,1024]{2,1,0:T(8,128)(2,1)S(1)} %copy-done.90, f32[768]{0:T(1024)S(1)} %fusion.175, f32[1024]{0:T(1024)S(1)} %bitcast.462), kind=kOutput, calls=%fused_computation.42 | convolution fusion | flops 3260545024 | bytes 15227904 | tf_op jit(solution)/shard_map/dot_general | solution.py:70
  156.5 9.2 %multiply_reduce_fusion.2 = (f32[1024]{0:T(1024)S(1)}, f32[768]{0:T(1024)S(1)}, f32[768]{0:T(1024)S(1)}, f32[1024]{0:T(1024)S(1)}, f32[768,1024]{1,0:T(8,128)}) fusion(f32[768]{0:T(1024)S(1)} %add_rsqrt_fusion.4, f32[768]{0:T(1024)S(1)} %broadcast_multiply_fusion.4, bf16[768,1024]{1,0:T(8,128)(2,1)S(1)} %get-tuple-element.76, f32[1024]{0:T(1024)S(1)} %bitcast.455, ...), kind=kOutput, calls=%fused_computation.87 | convolution fusion | flops 3232231936 | bytes 16805888 | tf_op jit(solution)/shard_map/dot_general | solution.py:70
  165.7 13.7 %convert_reduce_fusion.5 = (f32[1024]{0:T(1024)S(1)}, f32[1024]{0:T(1024)S(1)}, bf16[1,768,1024]{2,1,0:T(8,128)(2,1)}, f32[1024]{0:T(1024)S(1)}, bf16[768,1024]{1,0:T(8,128)(2,1)S(1)}, /*index=5*/f32[768,1024]{1,0:T(8,128)}) fusion(f32[1024]{0:T(1024)S(1)} %bitcast.463, f32[768]{0:T(1024)S(1)} %fusion.175, bf16[1,768,1024]{2,1,0:T(8,128)(2,1)S(1)} %copy-done.90, ...), kind=kOutput, calls=%fused_computation.86 | convolution fusion | flops 3259757568 | bytes 27839488 | tf_op jit(solution)/shard_map/dot_general | solution.py:70
  183.0 7.8 %fusion.222 = f32[8,768,768]{1,2,0:T(8,128)} fusion(bf16[768,8,64]{0,2,1:T(8,128)(2,1)S(1)} %bitcast.435, bf16[768,8,64]{0,2,1:T(8,128)(2,1)S(1)} %bitcast.434), kind=kOutput, calls=%fused_computation.334 | convolution fusion | flops 603979776 | bytes 20447232 | tf_op jit(solution)/shard_map/qhd,khd->hqk/dot_general | solution.py:110
  190.8 10.3 %convert_reduce_fusion.6 = (f32[8,64]{1,0:T(8,128)}, bf16[8,64,768]{2,1,0:T(8,128)(2,1)}) fusion(bf16[768,8,64]{0,2,1:T(8,128)(2,1)S(1)} %bitcast.436, f32[8,768,768]{1,2,0:T(8,128)} %get-tuple-element.74, f32[8,768]{1,0:T(8,128)S(1)} %log_add_fusion, pred[768,768]{0,1:T(8,128)(4,1)S(1)} %compare_and_fusion), kind=kOutput, calls=%fused_computation.153 | convolution fusion | flops 619314688 | bytes 21063680 | tf_op jit(solution)/shard_map/hqk,qhd->khd/dot_general | solution.py:111
  201.1 10.3 %convert_reduce_fusion.7 = (f32[8,64]{1,0:T(8,128)}, bf16[8,64,768]{2,1,0:T(8,128)(2,1)}) fusion(bf16[768,8,64]{0,2,1:T(8,128)(2,1)S(1)} %bitcast.429, f32[8,768,768]{1,2,0:T(8,128)} %fusion.140, f32[8,768]{1,0:T(8,128)S(1)} %log_add_fusion.1, pred[768,768]{0,1:T(8,128)(4,1)S(1)} %compare_and_fusion), kind=kOutput, calls=%fused_computation.154 | convolution fusion | flops 619314688 | bytes 21063680 | tf_op jit(solution)/shard_map/hqk,qhd->khd/dot_general | solution.py:111
  211.4 27.8 %multiply_reduce_fusion.1 = (f32[8,768]{1,0:T(8,128)S(1)}, f32[8,768]{1,0:T(8,128)S(1)}, f32[8,768,768]{1,2,0:T(8,128)}) fusion(f32[8,768,768]{1,2,0:T(8,128)} %fusion.140, f32[8,768]{1,0:T(8,128)S(1)} %log_add_fusion.1, pred[768,768]{0,1:T(8,128)(4,1)S(1)} %compare_and_fusion, f32[8,768,768]{1,2,0:T(8,128)} %fusion.222, f32[8,768]{1,0:T(8,128)S(1)} %log_add_fusion, ...), kind=kOutput, calls=%fused_computation.4 | convolution fusion | flops 641716224 | bytes 77758464 | tf_op jit(solution)/shard_map/qhd,khd->hqk/dot_general | solution.py:110
  239.2 25.2 %multiply_convert_fusion.1 = (bf16[8,768,768]{1,2,0:T(8,128)(2,1)S(1)}, bf16[8,768,768]{1,2,0:T(8,128)(2,1)S(1)}) fusion(f32[8,768,768]{1,2,0:T(8,128)} %get-tuple-element.78, f32[8,768,768]{1,2,0:T(8,128)} %fusion.140, f32[8,768]{1,0:T(8,128)S(1)} %get-tuple-element.29, f32[8,768]{1,0:T(8,128)S(1)} %log_add_fusion.1, pred[768,768]{0,1:T(8,128)(4,1)} %copy-done.17, ...), kind=kLoop, calls=%fused_computation.3 | loop fusion | flops 47185920 | bytes 95059968 | tf_op jit(solution)/shard_map/convert_element_type | solution.py:115
  268.8 6.1 fusion.60
  341.8 6.8 collective-permute-done.6
  355.2 6.5 convolution_convert_fusion
  362.2 6.2 fusion.183
  377.8 45.2 %all_gather.6 = f32[32,40,128]{2,1,0:T(8,128)S(1)} all-gather(f32[1,40,128]{2,1,0:T(8,128)S(1)} %pad_bitcast_fusion), channel_id=1, replica_groups=mesh['dp'=16,'mp'=2] {'dp','mp'}, dimensions={0}, use_global_device_ids=true | all-gather | bytes 675840 | tf_op jit(solution)/shard_map/all_gather | solution.py:264
  437.5 51.6 %reduce-scatter.5.cloned.1.call-done = bf16[3,64,512]{2,1,0:T(8,128)(2,1)} async-done(((bf16[3,1024,512]{2,1,0:T(8,128)(2,1)}), bf16[3,64,512]{2,1,0:T(8,128)(2,1)}) %reduce-scatter.5.cloned.1.call-update) | async-done | bytes 196624 | tf_op jit(solution)/shard_map/reduce_scatter | solution.py:128
  490.9 93.0 %reduce-scatter.9.cloned.1.call-done = bf16[64,2048]{1,0:T(8,128)(2,1)} async-done(((bf16[1024,2048]{1,0:T(8,128)(2,1)}), bf16[64,2048]{1,0:T(8,128)(2,1)}) %reduce-scatter.9.cloned.1.call-update) | async-done | bytes 262160 | tf_op jit(solution)/shard_map/reduce_scatter | solution.py:128
  585.7 95.3 %reduce-scatter.11.cloned.1.call-done = bf16[64,2048]{1,0:T(8,128)(2,1)} async-done(((bf16[1024,2048]{1,0:T(8,128)(2,1)}), bf16[64,2048]{1,0:T(8,128)(2,1)}) %reduce-scatter.11.cloned.1.call-update) | async-done | bytes 262160 | tf_op jit(solution)/shard_map/reduce_scatter | solution.py:128
  (376 shorter events, 168.4 us)
Async XLA Ops:
  8.0 417.0 %all-gather.2.cloned.1.call-start = ((), (), s32[]{:S(2)}) async-start(), calls=%async_computation.6 | async-start | bytes 1351680 | tf_op jit(solution)/shard_map/all_gather | solution.py:264
  9.0 34.6 %collective-permute-start.1 = (f32[3080]{0:T(1024)S(1)}, f32[3080]{0:T(1024)S(1)}, u32[]{:S(2)}, u32[]{:S(2)}) collective-permute-start(f32[3080]{0:T(1024)S(1)} %pad_maximum_fusion.3), channel_id=1, source_target_pairs={{0,1},{1,0},{2,3},{3,2},{4,5},{5,4},{6,7},{7,6},{8,9},{9,8},{10,11... | collective-permute-start | bytes 36968 | tf_op jit(solution)/shard_map/ppermute | solution.py:76
  14.1 29.6 %collective-permute-start = (bf16[4,1024,512]{2,1,0:T(8,128)(2,1)}, bf16[4,1024,512]{2,1,0:T(8,128)(2,1)}, u32[]{:S(2)}, u32[]{:S(2)}) collective-permute-start(bf16[4,1024,512]{2,1,0:T(8,128)(2,1)} %pad_maximum_fusion), channel_id=1, source_target_pairs={{0,1},{1,0},{2,3},{3,2},{4,5},{5,4},{6,7},{7,6},{8,9},{9,8},{10,11... | collective-permute-start | bytes 12582920 | tf_op jit(solution)/shard_map/ppermute | solution.py:76
  14.1 98.3 %collective-permute-start.2 = (bf16[1024,2048]{1,0:T(8,128)(2,1)}, bf16[1024,2048]{1,0:T(8,128)(2,1)}, u32[]{:S(2)}, u32[]{:S(2)}) collective-permute-start(bf16[1024,2048]{1,0:T(8,128)(2,1)} %param.28), channel_id=1, source_target_pairs={{0,1},{1,0},{2,3},{3,2},{4,5},{5,4},{6,7},{7,6},{8,9},{9,8},{10,11... | collective-permute-start | bytes 12582920 | tf_op jit(solution)/shard_map/ppermute | solution.py:76
  14.6 131.1 %collective-permute-start.3 = (bf16[1024,2048]{1,0:T(8,128)(2,1)}, bf16[1024,2048]{1,0:T(8,128)(2,1)}, u32[]{:S(2)}, u32[]{:S(2)}) collective-permute-start(bf16[1024,2048]{1,0:T(8,128)(2,1)} %param.30), channel_id=1, source_target_pairs={{0,1},{1,0},{2,3},{3,2},{4,5},{5,4},{6,7},{7,6},{8,9},{9,8},{10,11... | collective-permute-start | bytes 12582920 | tf_op jit(solution)/shard_map/ppermute | solution.py:76
  17.7 75.2 %copy-start.58 = (f32[768]{0:T(1024)}, f32[768]{0:T(1024)S(1)}, u32[]{:S(2)}) copy-start(f32[768]{0:T(1024)S(1)} %broadcast_multiply_fusion.5) | copy-start | bytes 9220
  19.7 73.2 %copy-start.63 = (f32[768]{0:T(1024)}, f32[768]{0:T(1024)S(1)}, u32[]{:S(2)}) copy-start(f32[768]{0:T(1024)S(1)} %add_rsqrt_fusion.5) | copy-start | bytes 9220
  29.5 63.4 %copy-start.61 = (f32[1,1024]{1,0:T(1,128)}, f32[1,1024]{1,0:T(1,128)S(1)}, u32[]{:S(2)}) copy-start(f32[1,1024]{1,0:T(1,128)S(1)} %get-tuple-element.50) | copy-start | bytes 12292
  29.5 63.4 %copy-start.78 = (f32[1,1024]{1,0:T(1,128)}, f32[1,1024]{1,0:T(1,128)S(1)}, u32[]{:S(2)}) copy-start(f32[1,1024]{1,0:T(1,128)S(1)} %get-tuple-element.49) | copy-start | bytes 12292
  29.5 136.1 %copy-start.76 = (f32[1,1024]{1,0:T(1,128)}, f32[1,1024]{1,0:T(1,128)S(1)}, u32[]{:S(2)}) copy-start(f32[1,1024]{1,0:T(1,128)S(1)} %get-tuple-element.46) | copy-start | bytes 12292
  33.4 177.9 %copy-start.17 = (pred[768,768]{0,1:T(8,128)(4,1)}, pred[768,768]{0,1:T(8,128)(4,1)S(1)}, u32[]{:S(2)}) copy-start(pred[768,768]{0,1:T(8,128)(4,1)S(1)} %compare_and_fusion) | copy-start | bytes 1769476
  43.6 122.1 %copy-start.80 = (f32[768]{0:T(1024)}, f32[768]{0:T(1024)S(1)}, u32[]{:S(2)}) copy-start(f32[768]{0:T(1024)S(1)} %fusion.175) | copy-start | bytes 9220
  43.6 122.0 %copy-start.74 = (f32[2048]{0:T(1024)}, f32[2048]{0:T(1024)S(1)}, u32[]{:S(2)}) copy-start(f32[2048]{0:T(1024)S(1)} %split.19) | copy-start | bytes 24580
  67.7 28.1 %slice-start.1 = ((s8[18874368]{0:T(1024)(128)(4,1)}), s8[4194304]{0:T(1024)(128)(4,1)S(1)}, s32[]{:S(2)}) async-start(s8[18874368]{0:T(1024)(128)(4,1)} %bitcast.391), calls=%async_computation.10 | async-start | bytes 8388608
  104.7 60.9 %copy-start.18 = (bf16[768,1024]{1,0:T(8,128)(2,1)}, bf16[768,1024]{1,0:T(8,128)(2,1)S(1)}, u32[]{:S(2)}) copy-start(bf16[768,1024]{1,0:T(8,128)(2,1)S(1)} %get-tuple-element.76) | copy-start | bytes 4718596
  310.3 125.8 %reduce-scatter.7.cloned.1.call-start = ((), (), s32[]{:S(2)}) async-start(), calls=%async_computation.5 | async-start | bytes 1114112 | tf_op jit(solution)/shard_map/reduce_scatter | solution.py:128
  314.0 10.0 %collective-permute-start.4 = (bf16[3,1024,512]{2,1,0:T(8,128)(2,1)}, bf16[3,1024,512]{2,1,0:T(8,128)(2,1)}, u32[]{:S(2)}, u32[]{:S(2)}) collective-permute-start(bf16[3,1024,512]{2,1,0:T(8,128)(2,1)} %pad_maximum_fusion.1), channel_id=1, source_target_pairs={{0,1},{1,0},{2,3},{3,2},{4,5},{5,4},{6,7},{7,6},{8,9},{9,8},{10,11... | collective-permute-start | bytes 9437192 | tf_op jit(solution)/shard_map/ppermute | solution.py:76
  315.5 5.9 collective-permute-start.5
  323.6 165.6 %reduce-scatter.5.cloned.1.call-start = ((), (), s32[]{:S(2)}) async-start(), calls=%async_computation.4 | async-start | bytes 3342336 | tf_op jit(solution)/shard_map/reduce_scatter | solution.py:128
  334.2 249.7 %reduce-scatter.9.cloned.1.call-start = ((), (), s32[]{:S(2)}) async-start(), calls=%async_computation.7 | async-start | bytes 4456448 | tf_op jit(solution)/shard_map/reduce_scatter | solution.py:128
  341.3 7.2 %collective-permute-start.6 = (bf16[1024,2048]{1,0:T(8,128)(2,1)S(1)}, bf16[1024,2048]{1,0:T(8,128)(2,1)S(1)}, u32[]{:S(2)}, u32[]{:S(2)}) collective-permute-start(bf16[1024,2048]{1,0:T(8,128)(2,1)S(1)} %convolution_convert_fusion.1), channel_id=1, source_target_pairs={{0,1},{1,0},{2,3},{3,2},{4,5},{5,4},{6,7},{7,6},{8,9},{9,8},{10,11... | collective-permute-start | bytes 12582920 | tf_op jit(solution)/shard_map/ppermute | solution.py:76
  353.8 327.2 %reduce-scatter.11.cloned.1.call-start = ((), (), s32[]{:S(2)}) async-start(), calls=%async_computation.8 | async-start | bytes 4456448 | tf_op jit(solution)/shard_map/reduce_scatter | solution.py:128
  361.7 7.8 %collective-permute-start.7 = (bf16[1024,2048]{1,0:T(8,128)(2,1)S(1)}, bf16[1024,2048]{1,0:T(8,128)(2,1)}, u32[]{:S(2)}, u32[]{:S(2)}) collective-permute-start(bf16[1024,2048]{1,0:T(8,128)(2,1)S(1)} %convolution_convert_fusion), channel_id=1, source_target_pairs={{0,1},{1,0},{2,3},{3,2},{4,5},{5,4},{6,7},{7,6},{8,9},{9,8},{10,11... | collective-permute-start | bytes 12582920 | tf_op jit(solution)/shard_map/ppermute | solution.py:76
  428.9 253.9 %copy-start.1 = (bf16[1024,1001]{0,1:T(8,128)(2,1)S(1)}, bf16[1024,1001]{0,1:T(8,128)(2,1)}, u32[]{:S(2)}) copy-start(bf16[1024,1001]{0,1:T(8,128)(2,1)} %param.34) | copy-start | bytes 6150148
  (98 other events, 533.0 us)
Sparse Core Ops, SparseCore 0:
  310.4 57.5 all-gather.1
Sparse Core Ops, SparseCore 1:
  323.6 81.6 reduce-scatter.6
  407.5 81.6 reduce-scatter.4
  491.3 92.5 reduce-scatter.8
  586.2 94.7 reduce-scatter.10
